TPU v7x, 32 devices: a whole 2x2x4 slice. The times are simulated.
32 devices in a mesh: rows: 16 (over z, y, x), rep: 2 (over core).
Axes of the slice: x: 2, y: 2, z: 4, core: 2. Of those that a mesh axis runs over, the one named last changes fastest.
Arguments:
- features: bfloat16 [4096, 128], P(('rows', 'rep')), may hold values from -6 to 6
- tile_counts: int32 [4096, 128, 128], P(('rows', 'rep')), may hold values from 0 to 3, as said below
- tile_row: int32 [4096], P(('rows', 'rep')), may hold values from 0 to 1
- tile_col: int32 [4096], P(('rows', 'rep')), may hold values from 0 to 31, as said below
- label_ids: int32 [2048], P(('rows', 'rep')), may hold values from 0 to 4095, as said below
- cotangent: bfloat16 [4096, 256], P(('rows', 'rep')), may hold values from -6 to 6
- self_weight: bfloat16 [128, 256], replicated, may hold values from -0.5 to 0.5
- neigh_weight: bfloat16 [128, 256], replicated, may hold values from -0.5 to 0.5
Outputs:
- activation: bfloat16 [4096, 256], P(('rows', 'rep'))
- grad_features: float32 [4096, 128], P(('rows', 'rep'))
- grad_self: float32 [128, 256], replicated
- grad_neigh: float32 [128, 256], replicated
Inputs may be any that keep to these rules, and one draw needn't show every extreme that they name: `tile_counts`: edge counts of one tile; most entries are zero. `tile_col`: every tile held by a device of rep index c names a column block of the feature rows of some device of rep index c. On each device, at most 16 tiles name column blocks held by devices of one rows index, and exactly 16 do for some rows index. `label_ids`: the ids of one device's 64 labels are distinct and lie among that device's own feature rows.
All inputs are finite; a program needn't handle non-finite values.
Results may differ from a plain program's by a relative error of at most 0.0053.
Values may be sent and summed in bfloat16 or wider, within the bound.
A program may use at most 128 MiB of HBM per device.

v0:
```python
import jax
import jax.numpy as jnp
from jax import lax
from jax.sharding import PartitionSpec as P

edge_moment = 14.0 / 96.0


def derivative(preact, masked):
    sigma = jax.nn.sigmoid(preact)
    return (masked.astype(jnp.float32) * sigma * (1.0 + preact * (1.0 - sigma))).astype(
        jnp.bfloat16
    )


def shards(
    features, tile_counts, tile_row, tile_col, label_ids, cotangent, self_weight, neigh_weight
):
    half_rows, width_in = features.shape
    block_size = tile_counts.shape[1]
    tile_total = tile_counts.shape[0]
    rep_count = lax.axis_size("rep")
    row_count = lax.axis_size("rows")
    per_half = half_rows // block_size
    row_blocks = rep_count * per_half
    scale = (edge_moment * tile_total * rep_count * block_size / row_blocks) ** (-0.5)
    gathered = lax.all_gather(features, "rows", axis=0, tiled=True)
    local_col = tile_col // (rep_count * per_half) * per_half + tile_col % per_half
    panels = gathered.reshape(-1, block_size, width_in)[local_col]
    counts = tile_counts.astype(jnp.bfloat16)
    products = jnp.einsum("tij,tjf->tif", counts, panels, preferred_element_type=jnp.float32)
    owner_table = (tile_row[:, None] == jnp.arange(row_blocks, dtype=jnp.int32)[None, :]).astype(
        jnp.float32
    )
    partial_rows = jnp.einsum(
        "tr,tif->rif", owner_table, products, precision=lax.Precision.HIGHEST
    ).reshape(row_blocks * block_size, width_in)
    local_ids = label_ids % half_rows
    label_mask = jnp.any(
        local_ids[:, None] == jnp.arange(half_rows, dtype=jnp.int32)[None, :], axis=0
    )
    masked = cotangent * label_mask[:, None].astype(jnp.bfloat16)
    rep_place = lax.axis_index("rep")
    neighbour_sum = lax.psum(partial_rows, "rep") * scale
    group_feat, group_masked = (
        lax.all_gather(features, "rep", axis=0, tiled=True),
        lax.all_gather(masked, "rep", axis=0, tiled=True),
    )
    neighbour = neighbour_sum.astype(jnp.bfloat16)
    preact = jnp.dot(group_feat, self_weight, preferred_element_type=jnp.float32) + jnp.dot(
        neighbour, neigh_weight, preferred_element_type=jnp.float32
    )
    activation_all = jax.nn.silu(preact).astype(jnp.bfloat16)
    delta_all = derivative(preact, group_masked)
    back = jnp.einsum(
        "nh,fh->nf", delta_all, neigh_weight, preferred_element_type=jnp.float32
    ).astype(jnp.bfloat16)
    activation = lax.dynamic_slice_in_dim(activation_all, rep_place * half_rows, half_rows, 0)
    delta_own = lax.dynamic_slice_in_dim(delta_all, rep_place * half_rows, half_rows, 0)
    neighbour_own = lax.dynamic_slice_in_dim(neighbour, rep_place * half_rows, half_rows, 0)
    self_part = jnp.einsum("nf,nh->fh", features, delta_own, preferred_element_type=jnp.float32)
    neigh_part = jnp.einsum(
        "nf,nh->fh", neighbour_own, delta_own, preferred_element_type=jnp.float32
    )
    pair_self, pair_neigh = lax.psum((self_part, neigh_part), "rep")
    self_total, neigh_total = lax.psum((pair_self, pair_neigh), "rows")
    grad_scale = float(label_ids.shape[0] * row_count * rep_count) ** (-0.5)
    picked = back.reshape(row_blocks, block_size, width_in)[tile_row]
    col_terms = jnp.einsum(
        "tij,tif->tjf", counts, picked, preferred_element_type=jnp.float32
    ).astype(jnp.bfloat16)
    count = half_rows * lax.axis_size("rows")
    block_count = count // block_size
    placing = (local_col[None, :] == jnp.arange(block_count, dtype=jnp.int32)[:, None]).astype(
        jnp.bfloat16
    )
    summed = jnp.einsum("bt,tif->bif", placing, col_terms, preferred_element_type=jnp.float32)
    scattered = lax.psum_scatter(
        summed.reshape(count, width_in), "rows", scatter_dimension=0, tiled=True
    )
    own_term = jnp.einsum("nh,fh->nf", delta_own, self_weight, preferred_element_type=jnp.float32)
    grad_features = own_term + scale * scattered
    return (activation, grad_features, grad_scale * self_total, grad_scale * neigh_total)


def solution(mesh):
    placed = (
        P(("rows", "rep"), None),
        P(("rows", "rep"), None, None),
        P(("rows", "rep")),
        P(("rows", "rep")),
        P(("rows", "rep")),
        P(("rows", "rep"), None),
        P(),
        P(),
    )
    return jax.shard_map(
        shards,
        mesh=mesh,
        in_specs=placed,
        out_specs=(P(("rows", "rep"), None), P(("rows", "rep"), None), P(), P()),
        check_vma=False,
    )
```

profile of v0, /device:TPU:0, one launch (start us, length us, event | category | flops | bytes accessed | tf_op | source)
XLA Modules:
  0.0 322.9 jit_solution(7102248980317323099)
XLA Ops:
  7.2 0.0 copy-start
  7.2 0.0 all-reduce.6.cloned.1.call-start
  7.2 0.7 compare_select_fusion.1
  7.9 45.6 %all_gather.10 = bf16[2048,128]{1,0:T(8,128)(2,1)S(1)} all-gather(bf16[128,128]{1,0:T(8,128)(2,1)} %param.8), channel_id=1, replica_groups=mesh['rows'=16,'rep'=2] {'rows'}, dimensions={0}, use_global_device_ids=true | all-gather | bytes 557056 | tf_op jit(solution)/shard_map/all_gather | solution.py:27
  53.5 3.1 gather_fusion
  56.5 11.0 %convolution_bitcast_fusion = f32[128,128,128]{1,2,0:T(8,128)} fusion(bf16[128,128,128]{2,1,0:T(8,128)(2,1)} %gather_fusion, s32[128,128,128]{2,1,0:T(8,128)} %param.9), kind=kOutput, calls=%fused_computation.3 | convolution fusion | flops 538968064 | bytes 20971520 | tf_op jit(solution)/shard_map/tij,tjf->tif/dot_general | solution.py:31
  67.5 9.3 %copy.29 = f32[128,128,128]{2,0,1:T(8,128)} copy(f32[128,128,128]{1,2,0:T(8,128)} %convolution_bitcast_fusion) | data formatting | bytes 16777216 | tf_op jit(solution)/shard_map/tij,tjf->tif/dot_general | solution.py:31
  76.8 0.0 copy-done.4
  76.8 0.0 copy-start.2
  76.8 0.0 copy-start.3
  76.8 6.2 %fusion.13 = f32[2,128,128]{2,0,1:T(2,128)S(1)} fusion(f32[128,128,128]{2,0,1:T(8,128)} %copy.29, s32[128]{0:T(128)S(1)} %copy-done.4), kind=kOutput, calls=%fused_computation.35 | convolution fusion | flops 50331904 | bytes 8520192 | tf_op jit(solution)/shard_map/tr,tif->rif/dot_general | solution.py:35
  83.0 0.7 copy.30
  83.7 0.0 all-reduce.6.cloned.1.call-update
  83.7 0.0 all-reduce.10.cloned.1.call-start
  83.8 0.0 copy-done.1
  83.8 1.9 all_gather.9
  85.6 0.0 copy-done.5
  85.6 0.1 fusion.8
  85.7 0.0 copy-done.2
  85.7 0.2 fusion.22
  85.9 0.0 copy-done.3
  85.9 0.1 broadcast_multiply_fusion.2
  86.0 1.9 all_gather.11
  87.9 9.7 %all-reduce.6.cloned.1.call-done = f32[256,128]{1,0:T(8,128)} async-done(((f32[256,128]{1,0:T(8,128)}), f32[256,128]{1,0:T(8,128)}) %all-reduce.6.cloned.1.call-update) | async-done | bytes 131088 | tf_op jit(solution)/shard_map/psum | solution.py:44
  97.6 0.9 multiply_convert_fusion.1
  98.6 0.0 copy-done
  98.6 0.3 multiply_convert_fusion
  98.8 0.9 fusion.3
  99.7 0.9 convolution_bitcast_fusion.1
  100.6 0.2 convolution_convert_fusion
  100.8 0.0 all-reduce.10.cloned.1.call-update
  100.8 0.0 all-reduce.8.cloned.1.call-start
  100.8 3.0 gather_fusion.1
  103.9 8.3 %convert_bitcast_fusion = bf16[128,128,128]{1,2,0:T(8,128)(2,1)} fusion(bf16[128,128,128]{2,1,0:T(8,128)(2,1)} %gather_fusion.1, s32[128,128,128]{2,1,0:T(8,128)} %param.9), kind=kOutput, calls=%fused_computation.2 | convolution fusion | flops 541065216 | bytes 16777216 | tf_op jit(solution)/shard_map/tij,tif->tjf/dot_general | solution.py:69
  112.2 6.7 %copy.32 = bf16[128,128,128]{2,0,1:T(8,128)(2,1)} copy(bf16[128,128,128]{1,2,0:T(8,128)(2,1)} %convert_bitcast_fusion) | data formatting | bytes 8388608 | tf_op jit(solution)/shard_map/convert_element_type | solution.py:71
  118.9 1.5 all-reduce.10.cloned.1.call-done
  120.4 0.0 all-reduce.8.cloned.1.call-update
  120.5 0.0 reduce-scatter.2.cloned.1.call-start
  120.5 2.8 fusion.10
  123.4 1.3 copy.33
  124.7 0.0 reduce-scatter.2.cloned.1.call-update
  124.7 0.7 fusion.2
  125.3 109.8 %all-reduce.8.cloned.1.call-done = (f32[128,256]{0,1:T(8,128)}, f32[128,256]{0,1:T(8,128)}) async-done(((f32[128,256]{0,1:T(8,128)}, f32[128,256]{0,1:T(8,128)}), (f32[128,256]{0,1:T(8,128)}, f32[128,256]{0,1:T(8,128)})) %all-reduce.8.cloned.1.call-update) | async-done | bytes 262160 | tf_op jit(solution)/shard_map/psum | solution.py:66
  235.1 1.0 broadcast_multiply_fusion
  236.1 0.8 copy.35
  236.9 0.8 copy.36
  237.6 77.1 %reduce-scatter.2.cloned.1.call-done = f32[128,128]{1,0:T(8,128)} async-done(((f32[2048,128]{1,0:T(8,128)}), f32[128,128]{1,0:T(8,128)}) %reduce-scatter.2.cloned.1.call-update) | async-done | bytes 65552 | tf_op jit(solution)/shard_map/reduce_scatter | solution.py:78
  314.8 1.6 convolution_add_fusion.1
  (8 shorter events, 0.0 us)
Async XLA Ops:
  7.2 91.4 %copy-start = (bf16[128,256]{1,0:T(8,128)(2,1)S(1)}, bf16[128,256]{1,0:T(8,128)(2,1)}, u32[]{:S(2)}) copy-start(bf16[128,256]{1,0:T(8,128)(2,1)} %param.15) | copy-start | bytes 196612
  7.2 90.5 %all-reduce.6.cloned.1.call-start = ((), (), s32[]{:S(2)}) async-start(), calls=%async_computation.1 | async-start | bytes 262144 | tf_op jit(solution)/shard_map/psum | solution.py:44
  67.5 9.3 %copy-start.4 = (s32[128]{0:T(128)S(1)}, s32[128]{0:T(128)}, u32[]{:S(2)}) copy-start(s32[128]{0:T(128)} %param.10) | copy-start | bytes 1540
  76.8 7.0 %copy-start.1 = (bf16[128,128]{1,0:T(8,128)(2,1)S(1)}, bf16[128,128]{1,0:T(8,128)(2,1)}, u32[]{:S(2)}) copy-start(bf16[128,128]{1,0:T(8,128)(2,1)} %param.8) | copy-start | bytes 98308
  76.8 8.9 %copy-start.5 = (s32[64]{0:T(128)S(1)}, s32[64]{0:T(128)}, u32[]{:S(2)}) copy-start(s32[64]{0:T(128)} %param.12) | copy-start | bytes 772
  76.8 9.0 %copy-start.2 = (bf16[128,256]{1,0:T(8,128)(2,1)S(1)}, bf16[128,256]{1,0:T(8,128)(2,1)}, u32[]{:S(2)}) copy-start(bf16[128,256]{1,0:T(8,128)(2,1)} %param.14) | copy-start | bytes 196612
  76.8 9.1 %copy-start.3 = (bf16[128,256]{1,0:T(8,128)(2,1)S(1)}, bf16[128,256]{1,0:T(8,128)(2,1)}, u32[]{:S(2)}) copy-start(bf16[128,256]{1,0:T(8,128)(2,1)} %param.13) | copy-start | bytes 196612
  83.7 36.7 %all-reduce.10.cloned.1.call-start = ((), (), s32[]{:S(2)}) async-start(), calls=%async_computation.4 | async-start | bytes 524288 | tf_op jit(solution)/shard_map/psum | solution.py:65
  100.8 134.3 %all-reduce.8.cloned.1.call-start = ((), (), s32[]{:S(2)}) async-start(), calls=%async_computation.3 | async-start | bytes 524288 | tf_op jit(solution)/shard_map/psum | solution.py:66
  120.5 194.3 %reduce-scatter.2.cloned.1.call-start = ((), (), s32[]{:S(2)}) async-start(), calls=%async_computation.2 | async-start | bytes 1114112 | tf_op jit(solution)/shard_map/reduce_scatter | solution.py:78
Sparse Core Ops, SparseCore 0:
  83.8 13.7 all-reduce.5
  100.9 19.4 all-reduce.9
  125.7 109.3 all-reduce.7
  237.2 77.4 reduce-scatter.1
where the time goes:
time: 323 us
  waiting for transfers between devices  198 us (61%)
  blocking collectives  49.3 us (15%)
  matrix products  32.3 us (10%)
  local copies, waits for them, and re-layouts  25.6 us (8%)
  between operations  13.9 us (4%)
  other arithmetic  3.44 us (1%)
    psum x1, waiting for transfers between devices, shards(): self_total, neigh_total = lax.psum((pair_self, pair_neigh), 'rows')  110 us
    reduce_scatter x1, waiting for transfers between devices, shards(): lax.psum_scatter(summed.reshape(count, width_in), 'rows', scatter_dimensi...  77.1 us
    all_gather x1, blocking collectives, shards(): gathered = lax.all_gather(features, 'rows', axis=0, tiled=True)  45.6 us
    dot_general x1, matrix products, shards(): jnp.einsum('tij,tjf->tif', counts, panels, preferred_element_type=jnp.flo...  11 us
    psum x1, waiting for transfers between devices, shards(): neighbour_sum = lax.psum(partial_rows, 'rep') * scale  9.71 us
    dot_general x1, local copies, waits for them, and re-layouts, shards(): jnp.einsum('tij,tjf->tif', counts, panels, preferred_element_type=jnp.flo...  9.29 us
    dot_general x1, matrix products, shards(): jnp.einsum('tij,tif->tjf', counts, picked, preferred_element_type=jnp.flo...  8.31 us
    convert_element_type x1, local copies, waits for them, and re-layouts, shards(): col_terms = jnp.einsum('tij,tif->tjf', counts, picked, preferred_element_...  6.75 us
  transfers between devices with their start and end apart: 4, of which 4 were waited for; matrix products, arithmetic and copies ran while one was open for 8% of the time, Pallas kernels for 0%

commit v1 on v0

v1 whole, which is shorter than its diff:
```python
import functools

import jax
import jax.numpy as jnp
from jax import lax
from jax.experimental import pallas as pl
from jax.experimental.pallas import tpu as pltpu
from jax.sharding import PartitionSpec as P

edge_moment = 14.0 / 96.0
MESH = pl.DeviceIdType.MESH
NT = (((1,), (1,)), ((), ()))
TN = (((0,), (0,)), ((), ()))


def dot(a, b, dims=(((1,), (0,)), ((), ()))):
    return lax.dot_general(a, b, dims, preferred_element_type=jnp.float32)


def build_kernel(row_s, col_s, counts_ref, a_ref, acc, *, per_step, rep_count, per_half, block):
    step = pl.program_id(0)

    @pl.when(step == 0)
    def _():
        acc[...] = jnp.zeros_like(acc)

    for u in range(per_step):
        t = step * per_step + u
        col = col_s[t]
        place = col // (rep_count * per_half) * per_half + col % per_half
        rows = pl.ds(pl.multiple_of(row_s[t] * block, block), block)
        acc[place, rows, :] += counts_ref[u]

    @pl.when(step == pl.num_programs(0) - 1)
    def _():
        def put(j, carry):
            cols = pl.ds(pl.multiple_of(j * block, block), block)
            a_ref[:, cols] = acc[j].astype(jnp.float32).astype(jnp.bfloat16)
            return carry

        lax.fori_loop(0, acc.shape[0], put, 0, unroll=4)


def build_adjacency(tile_counts, tile_row, tile_col, row_blocks, col_blocks, rep_count, per_half):
    tiles, block, _ = tile_counts.shape
    per_step = 16 if tiles % 16 == 0 else 1
    return pl.pallas_call(
        functools.partial(
            build_kernel, per_step=per_step, rep_count=rep_count, per_half=per_half, block=block
        ),
        out_shape=jax.ShapeDtypeStruct((row_blocks * block, col_blocks * block), jnp.bfloat16),
        grid_spec=pltpu.PrefetchScalarGridSpec(
            num_scalar_prefetch=2,
            grid=(tiles // per_step,),
            in_specs=[pl.BlockSpec((per_step, block, block), lambda s, r, c: (s, 0, 0))],
            out_specs=pl.BlockSpec(
                (row_blocks * block, col_blocks * block), lambda s, r, c: (0, 0)
            ),
            scratch_shapes=[pltpu.VMEM((col_blocks, row_blocks * block, block), jnp.int32)],
        ),
        compiler_params=pltpu.CompilerParams(dimension_semantics=("arbitrary",)),
        name="build_adjacency",
    )(tile_row, tile_col, tile_counts)


def layer_kernel(
    n, zs, ps, scale, grad_scale,
    feat, adj, ids, cot, ws, wn,
    act_out, grad_out, self_out, neigh_out,
    gath, part, part_in, bt, tt, r1, s2, r2, wpart, win, wc, wr1, wz, wo,
    ag_s, ag_r, pair_s, pair_r, r1_s, r1_r, r2_s, r2_r, w1_s, w1_r, wz_s, wz_r, wo_s, wo_r,
):
    me = lax.axis_index("rows")
    rep = lax.axis_index("rep")
    other = 1 - rep
    mz, mp = me // ps, me % ps
    half, f_in = feat.shape

    def zrow(d):
        return (mz + d) % zs

    def prow(d):
        return (mp + d) % ps

    def send(src, dst, ssem, rsem, row, core):
        copy = pltpu.make_async_remote_copy(
            src_ref=src, dst_ref=dst, send_sem=ssem, recv_sem=rsem,
            device_id=(row, core), device_id_type=MESH,
        )
        copy.start()
        sent.append(copy)
        return copy

    def arrived(dst, ssem, rsem):
        pltpu.make_async_remote_copy(
            src_ref=dst, dst_ref=dst, send_sem=ssem, recv_sem=rsem,
            device_id=(me, other), device_id_type=MESH,
        ).wait_recv()

    sent = []
    barrier = pltpu.get_barrier_semaphore()
    for d in range(1, zs):
        pl.semaphore_signal(barrier, inc=1, device_id=(zrow(d) * ps + mp, rep), device_id_type=MESH)
    for d in range(1, ps):
        pl.semaphore_signal(barrier, inc=1, device_id=(mz * ps + prow(d), rep), device_id_type=MESH)
    pl.semaphore_signal(barrier, inc=1, device_id=(me, other), device_id_type=MESH)
    pl.semaphore_wait(barrier, zs + ps - 1)

    for d in range(1, zs):
        send(feat, gath.at[me], ag_s.at[d - 1], ag_r.at[me], zrow(d) * ps + mp, rep)
    for d in range(1, ps):
        send(feat, gath.at[me], ag_s.at[zs - 2 + d], ag_r.at[me], mz * ps + prow(d), rep)
    gath[me] = feat[...]
    first = dot(feat[...], ws[...])
    near = lax.broadcasted_iota(jnp.int32, (half, ids.shape[1]), 0)
    hits = (near == ids[...] - (me * 2 + rep) * half).astype(jnp.float32)
    masked = cot[...].astype(jnp.float32) * jnp.max(hits, axis=1, keepdims=True)
    for e in range(1, zs):
        src = zrow(zs - e) * ps + mp
        arrived(gath.at[src], ag_s.at[0], ag_r.at[src])
        for d in range(1, ps):
            send(
                gath.at[src], gath.at[src], ag_s.at[zs - 2 + e * (ps - 1) + d], ag_r.at[src],
                mz * ps + prow(d), rep,
            )
    for e in range(zs):
        for d in range(1, ps):
            src = zrow(zs - e) * ps + prow(ps - d)
            arrived(gath.at[src], ag_s.at[0], ag_r.at[src])

    chunk = min(n, 16)
    cols = chunk * half

    def forward(c, total):
        left = adj[:, pl.ds(pl.multiple_of(c * cols, cols), cols)]
        right = gath[pl.ds(c * chunk, chunk)].reshape(cols, f_in)
        return total + dot(left, right)

    if n == chunk:
        total = dot(adj[...], gath[...].reshape(cols, f_in))
    else:
        total = lax.fori_loop(0, n // chunk, forward, jnp.zeros((2 * half, f_in), jnp.float32))
    part[...] = total.reshape(2, half, f_in)
    send(part.at[other], part_in, pair_s.at[0], pair_r.at[0], me, other)
    arrived(part_in, pair_s.at[0], pair_r.at[0])
    neighbour = (scale * (part[rep] + part_in[...])).astype(jnp.bfloat16)
    preact = first + dot(neighbour, wn[...])
    sigma = jax.nn.sigmoid(preact)
    act_out[...] = (preact * sigma).astype(jnp.bfloat16)
    delta = (masked * sigma * (1.0 + preact * (1.0 - sigma))).astype(jnp.bfloat16)
    bt[rep] = dot(wn[...], delta, NT).astype(jnp.bfloat16)
    send(bt.at[rep], bt.at[rep], pair_s.at[1], pair_r.at[1], me, other)
    wpart[0] = dot(feat[...], delta, TN)
    wpart[1] = dot(neighbour, delta, TN)
    send(wpart.at[other], win, pair_s.at[2], pair_r.at[2], me, other)
    own_term = dot(delta, ws[...], NT)

    arrived(bt.at[other], pair_s.at[1], pair_r.at[1])
    back = jnp.concatenate([bt[0], bt[1]], axis=1)

    def backward(c):
        out = dot(back, adj[:, pl.ds(pl.multiple_of(c * cols, cols), cols)])
        for j in range(chunk):
            tt[c * chunk + j] = out[:, j * half : (j + 1) * half].astype(jnp.bfloat16)

    if n == chunk:
        out = dot(back, adj[...])
        for j in range(n):
            tt[j] = out[:, j * half : (j + 1) * half].astype(jnp.bfloat16)
    else:
        pl.loop(0, n // chunk)(backward)

    arrived(win, pair_s.at[2], pair_r.at[2])
    wc[...] = (wpart[rep] + win[...]).reshape(wc.shape)
    for d in range(1, ps):
        send(
            wc.at[prow(d)], wr1.at[d - 1], w1_s.at[d - 1], w1_r.at[d - 1], mz * ps + prow(d), rep
        )
    for e in range(1, zs + 1):
        zt = zrow(e)
        for d in range(1, ps):
            k = zt * (ps - 1) + d - 1
            send(
                tt.at[zt * ps + prow(d)], r1.at[k], r1_s.at[(e - 1) * (ps - 1) + d - 1],
                r1_r.at[k], mz * ps + prow(d), rep,
            )
    shard = wc[mp]
    for d in range(1, ps):
        arrived(wr1.at[d - 1], w1_s.at[0], w1_r.at[d - 1])
        shard = shard + wr1[d - 1]
    wz[mz] = shard
    for d in range(1, zs):
        send(wz.at[mz], wz.at[mz], wz_s.at[d - 1], wz_r.at[mz], zrow(d) * ps + mp, rep)

    def plane_sum(zt):
        total = tt[zt * ps + mp].astype(jnp.float32)
        for d in range(1, ps):
            k = zt * (ps - 1) + d - 1
            arrived(r1.at[k], r1_s.at[0], r1_r.at[k])
            total = total + r1[k].astype(jnp.float32)
        return total

    for e in range(1, zs):
        s2[e - 1] = plane_sum(zrow(e)).astype(jnp.bfloat16)
        send(s2.at[e - 1], r2.at[e - 1], r2_s.at[e - 1], r2_r.at[e - 1], zrow(e) * ps + mp, rep)
    for d in range(1, zs):
        src = zrow(d)
        arrived(wz.at[src], wz_s.at[0], wz_r.at[src])
    shard = wz[0]
    for k in range(1, zs):
        shard = shard + wz[k]
    wo[rep, mp] = grad_scale * shard
    for d in range(1, ps):
        send(
            wo.at[rep, mp], wo.at[rep, mp], wo_s.at[d - 1], wo_r.at[mp], mz * ps + prow(d), rep
        )
    total = plane_sum(mz)
    for e in range(1, zs):
        arrived(r2.at[e - 1], r2_s.at[0], r2_r.at[e - 1])
        total = total + r2[e - 1].astype(jnp.float32)
    for d in range(1, ps):
        src = prow(d)
        arrived(wo.at[rep, src], wo_s.at[0], wo_r.at[src])
    send(wo.at[rep], wo.at[rep], pair_s.at[3], pair_r.at[3], me, other)
    grad_out[...] = own_term + scale * jnp.transpose(total)
    arrived(wo.at[other], pair_s.at[3], pair_r.at[3])
    self_out[...] = wo[0].reshape(self_out.shape)
    neigh_out[...] = wo[1].reshape(neigh_out.shape)
    for copy in sent:
        copy.wait_send()


def plane_size(n, width):
    return max(d for d in range(1, n + 1) if n % d == 0 and d * d <= 2 * n and width % (8 * d) == 0)


def shards(
    features, tile_counts, tile_row, tile_col, label_ids, cotangent, self_weight, neigh_weight
):
    half, f_in = features.shape
    hid = cotangent.shape[1]
    tile_total, block, _ = tile_counts.shape
    rep_count = lax.axis_size("rep")
    n = lax.axis_size("rows")
    per_half = half // block
    row_blocks = rep_count * per_half
    scale = (edge_moment * tile_total * rep_count * block / row_blocks) ** (-0.5)
    grad_scale = float(label_ids.shape[0] * n * rep_count) ** (-0.5)
    adj = build_adjacency(
        tile_counts, tile_row, tile_col, row_blocks, n * per_half, rep_count, per_half
    )
    ps = plane_size(n, f_in)
    zs = n // ps
    bf, f4 = jnp.bfloat16, jnp.float32
    dma = pltpu.SemaphoreType.DMA
    vmem = pl.BlockSpec(memory_space=pltpu.VMEM)
    return pl.pallas_call(
        functools.partial(layer_kernel, n, zs, ps, scale, grad_scale),
        out_shape=(
            jax.ShapeDtypeStruct((half, hid), bf),
            jax.ShapeDtypeStruct((half, f_in), f4),
            jax.ShapeDtypeStruct((f_in, hid), f4),
            jax.ShapeDtypeStruct((f_in, hid), f4),
        ),
        in_specs=[vmem] * 6,
        out_specs=(vmem,) * 4,
        scratch_shapes=[
            pltpu.VMEM((n, half, f_in), bf),
            pltpu.VMEM((2, half, f_in), f4),
            pltpu.VMEM((half, f_in), f4),
            pltpu.VMEM((2, f_in, half), bf),
            pltpu.VMEM((n, f_in, half), bf),
            pltpu.VMEM((zs * (ps - 1), f_in, half), bf),
            pltpu.VMEM((zs - 1, f_in, half), bf),
            pltpu.VMEM((zs - 1, f_in, half), bf),
            pltpu.VMEM((2, f_in, hid), f4),
            pltpu.VMEM((f_in, hid), f4),
            pltpu.VMEM((ps, f_in // ps, hid), f4),
            pltpu.VMEM((ps - 1, f_in // ps, hid), f4),
            pltpu.VMEM((zs, f_in // ps, hid), f4),
            pltpu.VMEM((2, ps, f_in // ps, hid), f4),
            dma((n,)), dma((n,)), dma((4,)), dma((4,)),
            dma((zs * (ps - 1),)), dma((zs * (ps - 1),)), dma((zs - 1,)), dma((zs - 1,)),
            dma((ps - 1,)), dma((ps - 1,)), dma((zs - 1,)), dma((zs,)),
            dma((ps - 1,)), dma((ps,)),
        ],
        compiler_params=pltpu.CompilerParams(
            collective_id=0, has_side_effects=True, vmem_limit_bytes=48 * 1024 * 1024
        ),
        name="layer",
    )(features, adj, label_ids.reshape(1, -1), cotangent, self_weight, neigh_weight)


def solution(mesh):
    placed = (
        P(("rows", "rep"), None),
        P(("rows", "rep"), None, None),
        P(("rows", "rep")),
        P(("rows", "rep")),
        P(("rows", "rep")),
        P(("rows", "rep"), None),
        P(),
        P(),
    )
    return jax.shard_map(
        shards,
        mesh=mesh,
        in_specs=placed,
        out_specs=(P(("rows", "rep"), None), P(("rows", "rep"), None), P(), P()),
        check_vma=False,
    )
```

time: 323 us -> 44.4 us (0.14)
  waiting for transfers between devices: 198 us -> 0 us
  blocking collectives: 49.3 us -> 0 us
  Pallas kernels: 0 us -> 39.6 us
  matrix products: 32.3 us -> 0 us
  local copies, waits for them, and re-layouts: 25.6 us -> 3.81 us
  between operations: 13.9 us -> 0.71 us
  other arithmetic: 3.44 us -> 0 us
    psum x3 -> x0, waiting for transfers between devices: 121 us -> none  [the longest x1 110 us: shards(): self_total, neigh_total = lax.psum((pair_self, pair_neigh), 'rows')]
    reduce_scatter x1 -> x0, waiting for transfers between devices: 77.1 us -> none  [shards(): lax.psum_scatter(summed.reshape(count, width_in), 'rows', scatter_dimensi...]
    all_gather x3 -> x0, blocking collectives: 49.3 us -> none  [the longest x1 45.6 us: shards(): gathered = lax.all_gather(features, 'rows', axis=0, tiled=True)]
    pallas_call x0 -> x2, Pallas kernels: none -> 39.6 us  [the longest x1 31.4 us: shards(): pl.pallas_call(functools.partial(layer_kernel, n, zs, ps, scale, grad_sca...]
    dot_general x10 -> x0, matrix products: 32.3 us -> none  [the longest x1 11 us: shards(): jnp.einsum('tij,tjf->tif', counts, panels, preferred_element_type=jnp.flo...]
    dot_general x3 -> x0, local copies, waits for them, and re-layouts: 11.3 us -> none  [the longest x1 9.29 us: shards(): jnp.einsum('tij,tjf->tif', counts, panels, preferred_element_type=jnp.flo...]
    convert_element_type x1 -> x0, local copies, waits for them, and re-layouts: 6.75 us -> none  [shards(): col_terms = jnp.einsum('tij,tif->tjf', counts, picked, preferred_element_...]
    gather x2 -> x0, local copies, waits for them, and re-layouts: 6.08 us -> none  [the longest x1 3.05 us: shards(): panels = gathered.reshape(-1, block_size, width_in)[local_col]]
  transfers between devices with their start and end apart: 4 -> 0, of which waited for: 4 -> 0; matrix products, arithmetic and copies ran while one was open for 8% -> 0% of each run, Pallas kernels for 0% -> 0%
where the time goes in v1:
time: 44.4 us; the launch traced here: 44.1 us
  Pallas kernels  39.6 us (89%)
  local copies, waits for them, and re-layouts  3.81 us (9%)
  between operations  0.71 us (2%)
    pallas_call x1, Pallas kernels, shards(): pl.pallas_call(functools.partial(layer_kernel, n, zs, ps, scale, grad_sca...  31.4 us
    pallas_call x1, Pallas kernels, build_adjacency(): pl.pallas_call(functools.partial(build_kernel, per_step=per_step, rep_cou...  8.2 us
    unnamed x16, local copies, waits for them, and re-layouts  3.81 us

profile of v1, /device:TPU:0, one launch (start us, length us, event | category | flops | bytes accessed | tf_op | source)
XLA Modules:
  0.0 44.1 jit_solution(3687471447676829994)
XLA Ops:
  0.6 0.0 copy-start.3
  0.6 0.0 copy-start.2
  0.7 0.0 copy-start.1
  0.7 0.0 copy-start.5
  0.7 0.0 copy-start.4
  0.7 8.2 %build_adjacency.1.adj = bf16[256,2048]{1,0:T(8,128)(2,1)} custom-call(s32[128]{0:T(128)} %row_s.1, s32[128]{0:T(128)} %col_s.1, s32[128,128,128]{2,1,0:T(8,128)} %counts_ref.1), custom_call_target="tpu_custom_call" | custom-call | tf_op jit(solution)/shard_map/build_adjacency/pallas_call | solution.py:47
  8.9 0.0 copy-done.3
  8.9 0.0 copy-done.2
  8.9 0.0 copy-done.1
  8.9 0.0 copy-done.5
  8.9 0.0 copy-done.4
  8.9 0.0 copy-start
  8.9 1.2 %copy-done = bf16[256,2048]{1,0:T(8,128)(2,1)S(1)} copy-done((bf16[256,2048]{1,0:T(8,128)(2,1)S(1)}, bf16[256,2048]{1,0:T(8,128)(2,1)}, u32[]{:S(2)}) %copy-start) | copy-done | bytes 1048600
  10.1 31.4 %layer.1 = (bf16[128,256]{1,0:T(8,128)(2,1)S(1)}, f32[128,128]{1,0:T(8,128)S(1)}, f32[128,256]{1,0:T(8,128)S(1)}, f32[128,256]{1,0:T(8,128)S(1)}) custom-call(bf16[128,128]{1,0:T(8,128)(2,1)S(1)} %copy-done.4, bf16[256,2048]{1,0:T(8,128)(2,1)S(1)} %copy-done, s32[1,64]{1,0:T(1,128)S(1)} %bitcast.1, bf16[128,256]{1,0:T(8,128)(2,1)S(1)} %copy-done.1, ...), custom_call_target="tpu_custom_call" | custom-call | tf_op jit(solution)/shard_map/layer/pallas_call | solution.py:257
  41.5 0.6 %copy.16 = bf16[128,256]{1,0:T(8,128)(2,1)} copy(bf16[128,256]{1,0:T(8,128)(2,1)S(1)} %get-tuple-element.8) | data formatting | bytes 131072
  42.1 0.6 %copy.17 = f32[128,128]{1,0:T(8,128)} copy(f32[128,128]{1,0:T(8,128)S(1)} %get-tuple-element.9) | data formatting | bytes 131072
  42.8 0.7 %copy.18 = f32[128,256]{1,0:T(8,128)} copy(f32[128,256]{1,0:T(8,128)S(1)} %get-tuple-element.10) | data formatting | bytes 262144
  43.4 0.7 %copy.19 = f32[128,256]{1,0:T(8,128)} copy(f32[128,256]{1,0:T(8,128)S(1)} %get-tuple-element.11) | data formatting | bytes 262144
Async XLA Ops:
  0.6 8.3 %copy-start.3 = (bf16[128,256]{1,0:T(8,128)(2,1)S(1)}, bf16[128,256]{1,0:T(8,128)(2,1)}, u32[]{:S(2)}) copy-start(bf16[128,256]{1,0:T(8,128)(2,1)} %wn.1) | copy-start | bytes 196612
  0.6 8.2 %copy-start.2 = (bf16[128,256]{1,0:T(8,128)(2,1)S(1)}, bf16[128,256]{1,0:T(8,128)(2,1)}, u32[]{:S(2)}) copy-start(bf16[128,256]{1,0:T(8,128)(2,1)} %ws.1) | copy-start | bytes 196612
  0.7 8.2 %copy-start.1 = (bf16[128,256]{1,0:T(8,128)(2,1)S(1)}, bf16[128,256]{1,0:T(8,128)(2,1)}, u32[]{:S(2)}) copy-start(bf16[128,256]{1,0:T(8,128)(2,1)} %cot.1) | copy-start | bytes 196612
  0.7 8.2 %copy-start.5 = (s32[64]{0:T(128)S(1)}, s32[64]{0:T(128)}, u32[]{:S(2)}) copy-start(s32[64]{0:T(128)} %param.12) | copy-start | bytes 772
  0.7 8.2 %copy-start.4 = (bf16[128,128]{1,0:T(8,128)(2,1)S(1)}, bf16[128,128]{1,0:T(8,128)(2,1)}, u32[]{:S(2)}) copy-start(bf16[128,128]{1,0:T(8,128)(2,1)} %feat.1) | copy-start | bytes 98308
  8.9 1.2 %copy-start = (bf16[256,2048]{1,0:T(8,128)(2,1)S(1)}, bf16[256,2048]{1,0:T(8,128)(2,1)}, u32[]{:S(2)}) copy-start(bf16[256,2048]{1,0:T(8,128)(2,1)} %build_adjacency.1.adj) | copy-start | bytes 3145732

commit v2 on v1

--- a/solution.py
+++ b/solution.py
@@ -17,50 +17,82 @@
     return lax.dot_general(a, b, dims, preferred_element_type=jnp.float32)
 
 
-def build_kernel(row_s, col_s, counts_ref, a_ref, acc, *, per_step, rep_count, per_half, block):
-    step = pl.program_id(0)
-
-    @pl.when(step == 0)
-    def _():
-        acc[...] = jnp.zeros_like(acc)
-
-    for u in range(per_step):
-        t = step * per_step + u
-        col = col_s[t]
-        place = col // (rep_count * per_half) * per_half + col % per_half
-        rows = pl.ds(pl.multiple_of(row_s[t] * block, block), block)
-        acc[place, rows, :] += counts_ref[u]
-
-    @pl.when(step == pl.num_programs(0) - 1)
-    def _():
-        def put(j, carry):
-            cols = pl.ds(pl.multiple_of(j * block, block), block)
-            a_ref[:, cols] = acc[j].astype(jnp.float32).astype(jnp.bfloat16)
-            return carry
-
-        lax.fori_loop(0, acc.shape[0], put, 0, unroll=4)
+def build_kernel(row_s, col_s, counts, a_ref, buf, acc, sems, *, rep_count, per_half, block):
+    parts = sems.shape[0]
+    size = buf.shape[0] // parts
+
+    def fetch(c):
+        span = pl.ds(c * size, size)
+        return pltpu.make_async_copy(counts.at[span], buf.at[span], sems.at[c])
+
+    for c in range(parts):
+        fetch(c).start()
+    acc[...] = jnp.zeros_like(acc)
+    group = 8 if size % 8 == 0 else 1
+    for c in range(parts):
+        fetch(c).wait()
+
+        @pl.loop(0, size // group)
+        def _(g):
+            for u in range(group):
+                t = c * size + g * group + u
+                col = col_s[t]
+                place = col // (rep_count * per_half) * per_half + col % per_half
+                rows = pl.ds(pl.multiple_of(row_s[t] * block, block), block)
+                acc[place, rows, :] += buf[t]
+
+    def put(j, carry):
+        cols = pl.ds(pl.multiple_of(j * block, block), block)
+        a_ref[:, cols] = acc[j].astype(jnp.float32).astype(jnp.bfloat16)
+        return carry
+
+    lax.fori_loop(0, acc.shape[0], put, 0, unroll=4)
 
 
 def build_adjacency(tile_counts, tile_row, tile_col, row_blocks, col_blocks, rep_count, per_half):
     tiles, block, _ = tile_counts.shape
-    per_step = 16 if tiles % 16 == 0 else 1
+    parts = 16 if tiles % 16 == 0 else 1
     return pl.pallas_call(
-        functools.partial(
-            build_kernel, per_step=per_step, rep_count=rep_count, per_half=per_half, block=block
-        ),
+        functools.partial(build_kernel, rep_count=rep_count, per_half=per_half, block=block),
         out_shape=jax.ShapeDtypeStruct((row_blocks * block, col_blocks * block), jnp.bfloat16),
         grid_spec=pltpu.PrefetchScalarGridSpec(
             num_scalar_prefetch=2,
-            grid=(tiles // per_step,),
-            in_specs=[pl.BlockSpec((per_step, block, block), lambda s, r, c: (s, 0, 0))],
-            out_specs=pl.BlockSpec(
-                (row_blocks * block, col_blocks * block), lambda s, r, c: (0, 0)
-            ),
-            scratch_shapes=[pltpu.VMEM((col_blocks, row_blocks * block, block), jnp.int32)],
+            grid=(),
+            in_specs=[pl.BlockSpec(memory_space=pl.ANY)],
+            out_specs=pl.BlockSpec(memory_space=pltpu.VMEM),
+            scratch_shapes=[
+                pltpu.VMEM((tiles, block, block), jnp.int32),
+                pltpu.VMEM((col_blocks, row_blocks * block, block), jnp.int32),
+                pltpu.SemaphoreType.DMA((parts,)),
+            ],
         ),
-        compiler_params=pltpu.CompilerParams(dimension_semantics=("arbitrary",)),
+        compiler_params=pltpu.CompilerParams(vmem_limit_bytes=59 * 1024 * 1024),
         name="build_adjacency",
     )(tile_row, tile_col, tile_counts)
+
+
+def finish_kernel(*refs):
+    count = len(refs) // 2
+    sems = refs[-1]
+    copies = [
+        pltpu.make_async_copy(refs[k], refs[count + k], sems.at[k]) for k in range(count)
+    ]
+    for copy in copies:
+        copy.start()
+    for copy in copies:
+        copy.wait()
+
+
+def finish(arrays):
+    return pl.pallas_call(
+        finish_kernel,
+        out_shape=tuple(jax.ShapeDtypeStruct(a.shape, a.dtype) for a in arrays),
+        in_specs=[pl.BlockSpec(memory_space=pltpu.VMEM)] * len(arrays),
+        out_specs=tuple(pl.BlockSpec(memory_space=pl.ANY) for _ in arrays),
+        scratch_shapes=[pltpu.SemaphoreType.DMA((len(arrays),))],
+        compiler_params=pltpu.CompilerParams(vmem_limit_bytes=4 * 1024 * 1024),
+        name="finish",
+    )(*arrays)
 
 
 def layer_kernel(
@@ -102,9 +134,12 @@
     for d in range(1, zs):
         pl.semaphore_signal(barrier, inc=1, device_id=(zrow(d) * ps + mp, rep), device_id_type=MESH)
     for d in range(1, ps):
-        pl.semaphore_signal(barrier, inc=1, device_id=(mz * ps + prow(d), rep), device_id_type=MESH)
+        for core in (rep, other):
+            pl.semaphore_signal(
+                barrier, inc=1, device_id=(mz * ps + prow(d), core), device_id_type=MESH
+            )
     pl.semaphore_signal(barrier, inc=1, device_id=(me, other), device_id_type=MESH)
-    pl.semaphore_wait(barrier, zs + ps - 1)
+    pl.semaphore_wait(barrier, zs + 2 * (ps - 1))
 
     for d in range(1, zs):
         send(feat, gath.at[me], ag_s.at[d - 1], ag_r.at[me], zrow(d) * ps + mp, rep)
@@ -123,23 +158,18 @@
                 gath.at[src], gath.at[src], ag_s.at[zs - 2 + e * (ps - 1) + d], ag_r.at[src],
                 mz * ps + prow(d), rep,
             )
+    span = ps * half
+
+    def plane_cols(zt):
+        return adj[:, pl.ds(pl.multiple_of(zt * span, span), span)]
+
+    total = jnp.zeros((2 * half, f_in), jnp.float32)
     for e in range(zs):
+        zt = zrow(zs - e)
         for d in range(1, ps):
-            src = zrow(zs - e) * ps + prow(ps - d)
+            src = zt * ps + prow(ps - d)
             arrived(gath.at[src], ag_s.at[0], ag_r.at[src])
-
-    chunk = min(n, 16)
-    cols = chunk * half
-
-    def forward(c, total):
-        left = adj[:, pl.ds(pl.multiple_of(c * cols, cols), cols)]
-        right = gath[pl.ds(c * chunk, chunk)].reshape(cols, f_in)
-        return total + dot(left, right)
-
-    if n == chunk:
-        total = dot(adj[...], gath[...].reshape(cols, f_in))
-    else:
-        total = lax.fori_loop(0, n // chunk, forward, jnp.zeros((2 * half, f_in), jnp.float32))
+        total = total + dot(plane_cols(zt), gath[pl.ds(zt * ps, ps)].reshape(span, f_in))
     part[...] = total.reshape(2, half, f_in)
     send(part.at[other], part_in, pair_s.at[0], pair_r.at[0], me, other)
     arrived(part_in, pair_s.at[0], pair_r.at[0])
@@ -158,37 +188,32 @@
     arrived(bt.at[other], pair_s.at[1], pair_r.at[1])
     back = jnp.concatenate([bt[0], bt[1]], axis=1)
 
-    def backward(c):
-        out = dot(back, adj[:, pl.ds(pl.multiple_of(c * cols, cols), cols)])
-        for j in range(chunk):
-            tt[c * chunk + j] = out[:, j * half : (j + 1) * half].astype(jnp.bfloat16)
-
-    if n == chunk:
-        out = dot(back, adj[...])
-        for j in range(n):
-            tt[j] = out[:, j * half : (j + 1) * half].astype(jnp.bfloat16)
-    else:
-        pl.loop(0, n // chunk)(backward)
-
-    arrived(win, pair_s.at[2], pair_r.at[2])
-    wc[...] = (wpart[rep] + win[...]).reshape(wc.shape)
-    for d in range(1, ps):
-        send(
-            wc.at[prow(d)], wr1.at[d - 1], w1_s.at[d - 1], w1_r.at[d - 1], mz * ps + prow(d), rep
-        )
-    for e in range(1, zs + 1):
+    def products(e):
         zt = zrow(e)
+        out = dot(back, plane_cols(zt))
+        for j in range(ps):
+            tt[zt * ps + j] = out[:, j * half : (j + 1) * half].astype(jnp.bfloat16)
         for d in range(1, ps):
             k = zt * (ps - 1) + d - 1
             send(
                 tt.at[zt * ps + prow(d)], r1.at[k], r1_s.at[(e - 1) * (ps - 1) + d - 1],
                 r1_r.at[k], mz * ps + prow(d), rep,
             )
-    shard = wc[mp]
+
+    products(1)
+    arrived(win, pair_s.at[2], pair_r.at[2])
+    wc[...] = (wpart[rep] + win[...]).astype(jnp.bfloat16).reshape(wc.shape)
+    for d in range(1, ps):
+        send(
+            wc.at[prow(d)], wr1.at[d - 1], w1_s.at[d - 1], w1_r.at[d - 1], mz * ps + prow(d), rep
+        )
+    for e in range(2, zs + 1):
+        products(e)
+    shard = wc[mp].astype(jnp.float32)
     for d in range(1, ps):
         arrived(wr1.at[d - 1], w1_s.at[0], w1_r.at[d - 1])
-        shard = shard + wr1[d - 1]
-    wz[mz] = shard
+        shard = shard + wr1[d - 1].astype(jnp.float32)
+    wz[mz] = shard.astype(jnp.bfloat16)
     for d in range(1, zs):
         send(wz.at[mz], wz.at[mz], wz_s.at[d - 1], wz_r.at[mz], zrow(d) * ps + mp, rep)
 
@@ -206,26 +231,29 @@
     for d in range(1, zs):
         src = zrow(d)
         arrived(wz.at[src], wz_s.at[0], wz_r.at[src])
-    shard = wz[0]
+    shard = wz[0].astype(jnp.float32)
     for k in range(1, zs):
-        shard = shard + wz[k]
-    wo[rep, mp] = grad_scale * shard
-    for d in range(1, ps):
-        send(
-            wo.at[rep, mp], wo.at[rep, mp], wo_s.at[d - 1], wo_r.at[mp], mz * ps + prow(d), rep
-        )
+        shard = shard + wz[k].astype(jnp.float32)
+    wo[rep, mp] = (grad_scale * shard).astype(jnp.bfloat16)
+    send(wo.at[rep, mp], wo.at[rep, mp], wo_s.at[0], wo_r.at[rep, mp], me, other)
+    for d in range(1, ps):
+        for c, core in enumerate((rep, other)):
+            send(
+                wo.at[rep, mp], wo.at[rep, mp], wo_s.at[2 * d - 1 + c], wo_r.at[rep, mp],
+                mz * ps + prow(d), core,
+            )
     total = plane_sum(mz)
     for e in range(1, zs):
         arrived(r2.at[e - 1], r2_s.at[0], r2_r.at[e - 1])
         total = total + r2[e - 1].astype(jnp.float32)
+    grad_out[...] = own_term + scale * jnp.transpose(total)
+    arrived(wo.at[other, mp], wo_s.at[0], wo_r.at[other, mp])
     for d in range(1, ps):
         src = prow(d)
-        arrived(wo.at[rep, src], wo_s.at[0], wo_r.at[src])
-    send(wo.at[rep], wo.at[rep], pair_s.at[3], pair_r.at[3], me, other)
-    grad_out[...] = own_term + scale * jnp.transpose(total)
-    arrived(wo.at[other], pair_s.at[3], pair_r.at[3])
-    self_out[...] = wo[0].reshape(self_out.shape)
-    neigh_out[...] = wo[1].reshape(neigh_out.shape)
+        for core in (rep, other):
+            arrived(wo.at[core, src], wo_s.at[0], wo_r.at[core, src])
+    self_out[...] = wo[0].astype(jnp.float32).reshape(self_out.shape)
+    neigh_out[...] = wo[1].astype(jnp.float32).reshape(neigh_out.shape)
     for copy in sent:
         copy.wait_send()
 
@@ -254,7 +282,7 @@
     bf, f4 = jnp.bfloat16, jnp.float32
     dma = pltpu.SemaphoreType.DMA
     vmem = pl.BlockSpec(memory_space=pltpu.VMEM)
-    return pl.pallas_call(
+    outs = pl.pallas_call(
         functools.partial(layer_kernel, n, zs, ps, scale, grad_scale),
         out_shape=(
             jax.ShapeDtypeStruct((half, hid), bf),
@@ -275,20 +303,21 @@
             pltpu.VMEM((zs - 1, f_in, half), bf),
             pltpu.VMEM((2, f_in, hid), f4),
             pltpu.VMEM((f_in, hid), f4),
-            pltpu.VMEM((ps, f_in // ps, hid), f4),
-            pltpu.VMEM((ps - 1, f_in // ps, hid), f4),
-            pltpu.VMEM((zs, f_in // ps, hid), f4),
-            pltpu.VMEM((2, ps, f_in // ps, hid), f4),
-            dma((n,)), dma((n,)), dma((4,)), dma((4,)),
+            pltpu.VMEM((ps, f_in // ps, hid), bf),
+            pltpu.VMEM((ps - 1, f_in // ps, hid), bf),
+            pltpu.VMEM((zs, f_in // ps, hid), bf),
+            pltpu.VMEM((2, ps, f_in // ps, hid), bf),
+            dma((n,)), dma((n,)), dma((3,)), dma((3,)),
             dma((zs * (ps - 1),)), dma((zs * (ps - 1),)), dma((zs - 1,)), dma((zs - 1,)),
             dma((ps - 1,)), dma((ps - 1,)), dma((zs - 1,)), dma((zs,)),
-            dma((ps - 1,)), dma((ps,)),
+            dma((2 * ps - 1,)), dma((2, ps)),
         ],
         compiler_params=pltpu.CompilerParams(
             collective_id=0, has_side_effects=True, vmem_limit_bytes=48 * 1024 * 1024
         ),
         name="layer",
     )(features, adj, label_ids.reshape(1, -1), cotangent, self_weight, neigh_weight)
+    return finish(outs)
 
 
 def solution(mesh):

time: 44.4 us -> 39 us (0.88)
  Pallas kernels: 39.6 us -> 36.8 us
  local copies, waits for them, and re-layouts: 3.81 us -> 1.24 us
    unnamed x16 -> x12, local copies, waits for them, and re-layouts: 3.81 us -> 1.24 us
    pallas_call x1 -> x2, Pallas kernels: 8.2 us -> 6.4 us  [the longest x1 5.62 us: build_adjacency(): pl.pallas_call(functools.partial(build_kernel, rep_count=rep_count, per_h...]
    pallas_call x1, Pallas kernels: 31.4 us -> 30.4 us  [shards(): pl.pallas_call(functools.partial(layer_kernel, n, zs, ps, scale, grad_sca...]
where the time goes in v2:
time: 39 us; the launch traced here: 38.8 us
  Pallas kernels  36.8 us (94%)
  local copies, waits for them, and re-layouts  1.24 us (3%)
  between operations  0.74 us (2%)
    pallas_call x1, Pallas kernels, shards(): pl.pallas_call(functools.partial(layer_kernel, n, zs, ps, scale, grad_sca...  30.4 us
    pallas_call x1, Pallas kernels, build_adjacency(): pl.pallas_call(functools.partial(build_kernel, rep_count=rep_count, per_h...  5.62 us
    unnamed x12, local copies, waits for them, and re-layouts  1.24 us

profile of v2, /device:TPU:0, one launch (start us, length us, event | category | flops | bytes accessed | tf_op | source)
XLA Modules:
  0.0 38.8 jit_solution(5519026200574048580)
XLA Ops:
  0.6 0.0 copy-start.3
  0.6 0.0 copy-start.2
  0.7 0.0 copy-start.1
  0.7 0.0 copy-start.5
  0.7 0.0 copy-start.4
  0.7 5.6 %build_adjacency.1.adj = bf16[256,2048]{1,0:T(8,128)(2,1)} custom-call(s32[128]{0:T(128)} %row_s.1, s32[128]{0:T(128)} %col_s.1, s32[128,128,128]{2,1,0:T(8,128)} %counts.1), custom_call_target="tpu_custom_call" | custom-call | tf_op jit(solution)/shard_map/build_adjacency/pallas_call | solution.py:55
  6.3 0.0 copy-done.3
  6.3 0.0 copy-done.2
  6.3 0.0 copy-done.1
  6.3 0.0 copy-done.5
  6.3 0.0 copy-done.4
  6.4 0.0 copy-start
  6.4 1.2 %copy-done = bf16[256,2048]{1,0:T(8,128)(2,1)S(1)} copy-done((bf16[256,2048]{1,0:T(8,128)(2,1)S(1)}, bf16[256,2048]{1,0:T(8,128)(2,1)}, u32[]{:S(2)}) %copy-start) | copy-done | bytes 1048600
  7.6 30.4 %layer.1 = (bf16[128,256]{1,0:T(8,128)(2,1)S(1)}, f32[128,128]{1,0:T(8,128)S(1)}, f32[128,256]{1,0:T(8,128)S(1)}, f32[128,256]{1,0:T(8,128)S(1)}) custom-call(bf16[128,128]{1,0:T(8,128)(2,1)S(1)} %copy-done.4, bf16[256,2048]{1,0:T(8,128)(2,1)S(1)} %copy-done, s32[1,64]{1,0:T(1,128)S(1)} %bitcast.1, bf16[128,256]{1,0:T(8,128)(2,1)S(1)} %copy-done.1, ...), custom_call_target="tpu_custom_call" | custom-call | tf_op jit(solution)/shard_map/layer/pallas_call | solution.py:285
  38.0 0.8 %finish.1 = (bf16[128,256]{1,0:T(8,128)(2,1)}, f32[128,128]{1,0:T(8,128)}, f32[128,256]{1,0:T(8,128)}, f32[128,256]{1,0:T(8,128)}) custom-call(bf16[128,256]{1,0:T(8,128)(2,1)S(1)} %get-tuple-element.8.refs_0_, f32[128,128]{1,0:T(8,128)S(1)} %get-tuple-element.9.refs_1_, f32[128,256]{1,0:T(8,128)S(1)} %get-tuple-element.10.refs_2_, ...), custom_call_target="tpu_custom_call" | custom-call | tf_op jit(solution)/shard_map/finish/pallas_call | solution.py:87
Async XLA Ops:
  0.6 5.7 %copy-start.3 = (bf16[128,256]{1,0:T(8,128)(2,1)S(1)}, bf16[128,256]{1,0:T(8,128)(2,1)}, u32[]{:S(2)}) copy-start(bf16[128,256]{1,0:T(8,128)(2,1)} %wn.1) | copy-start | bytes 196612
  0.6 5.7 %copy-start.2 = (bf16[128,256]{1,0:T(8,128)(2,1)S(1)}, bf16[128,256]{1,0:T(8,128)(2,1)}, u32[]{:S(2)}) copy-start(bf16[128,256]{1,0:T(8,128)(2,1)} %ws.1) | copy-start | bytes 196612
  0.7 5.7 %copy-start.1 = (bf16[128,256]{1,0:T(8,128)(2,1)S(1)}, bf16[128,256]{1,0:T(8,128)(2,1)}, u32[]{:S(2)}) copy-start(bf16[128,256]{1,0:T(8,128)(2,1)} %cot.1) | copy-start | bytes 196612
  0.7 5.7 %copy-start.5 = (s32[64]{0:T(128)S(1)}, s32[64]{0:T(128)}, u32[]{:S(2)}) copy-start(s32[64]{0:T(128)} %param.12) | copy-start | bytes 772
  0.7 5.7 %copy-start.4 = (bf16[128,128]{1,0:T(8,128)(2,1)S(1)}, bf16[128,128]{1,0:T(8,128)(2,1)}, u32[]{:S(2)}) copy-start(bf16[128,128]{1,0:T(8,128)(2,1)} %feat.1) | copy-start | bytes 98308
  6.4 1.2 %copy-start = (bf16[256,2048]{1,0:T(8,128)(2,1)S(1)}, bf16[256,2048]{1,0:T(8,128)(2,1)}, u32[]{:S(2)}) copy-start(bf16[256,2048]{1,0:T(8,128)(2,1)} %build_adjacency.1.adj) | copy-start | bytes 3145732

commit v3 on v2

--- a/solution.py
+++ b/solution.py
@@ -17,58 +17,41 @@
     return lax.dot_general(a, b, dims, preferred_element_type=jnp.float32)
 
 
-def build_kernel(row_s, col_s, counts, a_ref, buf, acc, sems, *, rep_count, per_half, block):
-    parts = sems.shape[0]
-    size = buf.shape[0] // parts
-
-    def fetch(c):
-        span = pl.ds(c * size, size)
-        return pltpu.make_async_copy(counts.at[span], buf.at[span], sems.at[c])
-
-    for c in range(parts):
-        fetch(c).start()
-    acc[...] = jnp.zeros_like(acc)
-    group = 8 if size % 8 == 0 else 1
-    for c in range(parts):
-        fetch(c).wait()
-
-        @pl.loop(0, size // group)
-        def _(g):
-            for u in range(group):
-                t = c * size + g * group + u
-                col = col_s[t]
-                place = col // (rep_count * per_half) * per_half + col % per_half
-                rows = pl.ds(pl.multiple_of(row_s[t] * block, block), block)
-                acc[place, rows, :] += buf[t]
-
-    def put(j, carry):
-        cols = pl.ds(pl.multiple_of(j * block, block), block)
-        a_ref[:, cols] = acc[j].astype(jnp.float32).astype(jnp.bfloat16)
-        return carry
-
-    lax.fori_loop(0, acc.shape[0], put, 0, unroll=4)
-
-
-def build_adjacency(tile_counts, tile_row, tile_col, row_blocks, col_blocks, rep_count, per_half):
-    tiles, block, _ = tile_counts.shape
-    parts = 16 if tiles % 16 == 0 else 1
+def table_kernel(row_s, col_s, table, filled, *, rep_count, cap):
+    tiles = row_s.shape[0]
+    group = 8 if tiles % 8 == 0 else 1
+
+    @pl.loop(0, filled.shape[0])
+    def _(j):
+        filled[j] = 0
+        for k in range(cap):
+            table[j * cap + k] = 2 * tiles
+
+    @pl.loop(0, tiles // group)
+    def _(g):
+        for u in range(group):
+            t = g * group + u
+            owner = col_s[t] // rep_count
+            have = filled[owner]
+            table[owner * cap + have] = 2 * t + row_s[t]
+            filled[owner] = have + 1
+
+
+def slot_table(tile_row, tile_col, n, rep_count, cap):
     return pl.pallas_call(
-        functools.partial(build_kernel, rep_count=rep_count, per_half=per_half, block=block),
-        out_shape=jax.ShapeDtypeStruct((row_blocks * block, col_blocks * block), jnp.bfloat16),
+        functools.partial(table_kernel, rep_count=rep_count, cap=cap),
+        out_shape=jax.ShapeDtypeStruct((n * cap,), jnp.int32),
         grid_spec=pltpu.PrefetchScalarGridSpec(
             num_scalar_prefetch=2,
             grid=(),
-            in_specs=[pl.BlockSpec(memory_space=pl.ANY)],
-            out_specs=pl.BlockSpec(memory_space=pltpu.VMEM),
-            scratch_shapes=[
-                pltpu.VMEM((tiles, block, block), jnp.int32),
-                pltpu.VMEM((col_blocks, row_blocks * block, block), jnp.int32),
-                pltpu.SemaphoreType.DMA((parts,)),
-            ],
+            in_specs=[],
+            out_specs=pl.BlockSpec(memory_space=pltpu.SMEM),
+            scratch_shapes=[pltpu.SMEM((n,), jnp.int32)],
         ),
-        compiler_params=pltpu.CompilerParams(vmem_limit_bytes=59 * 1024 * 1024),
-        name="build_adjacency",
-    )(tile_row, tile_col, tile_counts)
+        compiler_params=pltpu.CompilerParams(vmem_limit_bytes=60 * 1024 * 1024),
+        cost_estimate=pl.CostEstimate(flops=1 << 33, bytes_accessed=1 << 24, transcendentals=0),
+        name="slot_table",
+    )(tile_row, tile_col)
 
 
 def finish_kernel(*refs):
@@ -96,11 +79,11 @@
 
 
 def layer_kernel(
-    n, zs, ps, scale, grad_scale,
-    feat, adj, ids, cot, ws, wn,
+    n, zs, ps, cap, scale, grad_scale,
+    table, counts, feat, ids, cot, ws, wn,
     act_out, grad_out, self_out, neigh_out,
-    gath, part, part_in, bt, tt, r1, s2, r2, wpart, win, wc, wr1, wz, wo,
-    ag_s, ag_r, pair_s, pair_r, r1_s, r1_r, r2_s, r2_r, w1_s, w1_r, wz_s, wz_r, wo_s, wo_r,
+    buf, adj, gath, part, part_in, bt, tt, r1, s2, r2, wpart, win, wc, wr1, wz, wo,
+    ag_s, ag_r, pair_s, pair_r, r1_s, r1_r, r2_s, r2_r, w1_s, w1_r, wz_s, wz_r, wo_s, wo_r, tile_s,
 ):
     me = lax.axis_index("rows")
     rep = lax.axis_index("rep")
@@ -130,6 +113,17 @@
         ).wait_recv()
 
     sent = []
+    tiles = counts.shape[0]
+    parts = tile_s.shape[0]
+    size = tiles // parts
+    fetches = []
+    for c in range(parts):
+        fetches.append(
+            pltpu.make_async_copy(
+                counts.at[pl.ds(c * size, size)], buf.at[pl.ds(c * size, size)], tile_s.at[c]
+            )
+        )
+        fetches[-1].start()
     barrier = pltpu.get_barrier_semaphore()
     for d in range(1, zs):
         pl.semaphore_signal(barrier, inc=1, device_id=(zrow(d) * ps + mp, rep), device_id_type=MESH)
@@ -150,7 +144,9 @@
     near = lax.broadcasted_iota(jnp.int32, (half, ids.shape[1]), 0)
     hits = (near == ids[...] - (me * 2 + rep) * half).astype(jnp.float32)
     masked = cot[...].astype(jnp.float32) * jnp.max(hits, axis=1, keepdims=True)
-    for e in range(1, zs):
+    buf[tiles] = jnp.zeros((half, half), jnp.int32)
+
+    def pass_on(e):
         src = zrow(zs - e) * ps + mp
         arrived(gath.at[src], ag_s.at[0], ag_r.at[src])
         for d in range(1, ps):
@@ -158,6 +154,30 @@
                 gath.at[src], gath.at[src], ag_s.at[zs - 2 + e * (ps - 1) + d], ag_r.at[src],
                 mz * ps + prow(d), rep,
             )
+
+    def build_plane(zt):
+        @pl.loop(0, ps)
+        def _(q):
+            j = zt * ps + q
+            both = jnp.zeros((half, half), jnp.int32)
+            low = both
+            for k in range(cap):
+                entry = table[j * cap + k]
+                tile = buf[entry // 2]
+                both = both + tile
+                low = low + tile * (entry % 2)
+            cols = pl.ds(pl.multiple_of(j * half, half), half)
+            adj[:half, cols] = (both - low).astype(jnp.float32).astype(jnp.bfloat16)
+            adj[half:, cols] = low.astype(jnp.float32).astype(jnp.bfloat16)
+
+    pass_on(1)
+    for fetch in fetches:
+        fetch.wait()
+    for e in range(zs):
+        build_plane(zrow(zs - e))
+        if 2 <= e + 2 < zs:
+            pass_on(e + 2)
+
     span = ps * half
 
     def plane_cols(zt):
@@ -274,25 +294,28 @@
     row_blocks = rep_count * per_half
     scale = (edge_moment * tile_total * rep_count * block / row_blocks) ** (-0.5)
     grad_scale = float(label_ids.shape[0] * n * rep_count) ** (-0.5)
-    adj = build_adjacency(
-        tile_counts, tile_row, tile_col, row_blocks, n * per_half, rep_count, per_half
-    )
+    cap = tile_total * rep_count // n
+    parts = 8 if tile_total % 8 == 0 else 1
+    table = slot_table(tile_row, tile_col, n, rep_count, cap)
     ps = plane_size(n, f_in)
     zs = n // ps
     bf, f4 = jnp.bfloat16, jnp.float32
     dma = pltpu.SemaphoreType.DMA
     vmem = pl.BlockSpec(memory_space=pltpu.VMEM)
     outs = pl.pallas_call(
-        functools.partial(layer_kernel, n, zs, ps, scale, grad_scale),
+        functools.partial(layer_kernel, n, zs, ps, cap, scale, grad_scale),
         out_shape=(
             jax.ShapeDtypeStruct((half, hid), bf),
             jax.ShapeDtypeStruct((half, f_in), f4),
             jax.ShapeDtypeStruct((f_in, hid), f4),
             jax.ShapeDtypeStruct((f_in, hid), f4),
         ),
-        in_specs=[vmem] * 6,
+        in_specs=[pl.BlockSpec(memory_space=pltpu.SMEM), pl.BlockSpec(memory_space=pl.ANY)]
+        + [vmem] * 5,
         out_specs=(vmem,) * 4,
         scratch_shapes=[
+            pltpu.VMEM((tile_total + 1, block, block), jnp.int32),
+            pltpu.VMEM((row_blocks * block, n * block), bf),
             pltpu.VMEM((n, half, f_in), bf),
             pltpu.VMEM((2, half, f_in), f4),
             pltpu.VMEM((half, f_in), f4),
@@ -310,13 +333,13 @@
             dma((n,)), dma((n,)), dma((3,)), dma((3,)),
             dma((zs * (ps - 1),)), dma((zs * (ps - 1),)), dma((zs - 1,)), dma((zs - 1,)),
             dma((ps - 1,)), dma((ps - 1,)), dma((zs - 1,)), dma((zs,)),
-            dma((2 * ps - 1,)), dma((2, ps)),
+            dma((2 * ps - 1,)), dma((2, ps)), dma((parts,)),
         ],
         compiler_params=pltpu.CompilerParams(
-            collective_id=0, has_side_effects=True, vmem_limit_bytes=48 * 1024 * 1024
+            collective_id=0, has_side_effects=True, vmem_limit_bytes=50 * 1024 * 1024
         ),
         name="layer",
-    )(features, adj, label_ids.reshape(1, -1), cotangent, self_weight, neigh_weight)
+    )(table, tile_counts, features, label_ids.reshape(1, -1), cotangent, self_weight, neigh_weight)
     return finish(outs)
 
 

time: 39 us -> 36.1 us (0.926)
  Pallas kernels: 36.8 us -> 34.5 us
  local copies, waits for them, and re-layouts: 1.24 us -> 0.7 us
    pallas_call x2, Pallas kernels: 36 us -> 33.7 us  [the longest x1 31.1 us: shards(): pl.pallas_call(functools.partial(layer_kernel, n, zs, ps, cap, scale, gra...]
    unnamed x12, local copies, waits for them, and re-layouts: 1.24 us -> 0.7 us
where the time goes in v3:
time: 36.1 us; the launch traced here: 35.9 us
  Pallas kernels  34.5 us (96%)
  between operations  0.74 us (2%)
  local copies, waits for them, and re-layouts  0.7 us (2%)
    pallas_call x1, Pallas kernels, shards(): pl.pallas_call(functools.partial(layer_kernel, n, zs, ps, cap, scale, gra...  31.1 us
    pallas_call x1, Pallas kernels, slot_table(): pl.pallas_call(functools.partial(table_kernel, rep_count=rep_count, cap=c...  2.67 us
    pallas_call x1, Pallas kernels, finish(): pl.pallas_call(finish_kernel, out_shape=tuple((jax.ShapeDtypeStruct(a.sha...  0.78 us

profile of v3, /device:TPU:0, one launch (start us, length us, event | category | flops | bytes accessed | tf_op | source)
XLA Modules:
  0.0 35.9 jit_solution(4460060294827090123)
XLA Ops:
  0.6 0.0 copy-start
  0.6 0.0 copy-start.1
  0.7 0.0 copy-start.2
  0.7 0.0 copy-start.3
  0.7 0.0 copy-start.5
  0.7 2.7 %slot_table.1.table = s32[256]{0:T(256)} custom-call(s32[128]{0:T(128)} %row_s.1, s32[128]{0:T(128)} %col_s.1), custom_call_target="tpu_custom_call" | custom-call | flops 8589934592 | bytes 16777216 | tf_op jit(solution)/shard_map/slot_table/pallas_call | solution.py:41
  3.4 0.0 copy-done
  3.4 0.0 copy-done.1
  3.4 0.0 copy-done.2
  3.4 0.0 copy-done.3
  3.4 0.0 copy-done.5
  3.4 0.0 copy-start.4
  3.4 0.7 %copy-done.4 = s32[256]{0:T(256)S(1)} copy-done((s32[256]{0:T(256)S(1)}, s32[256]{0:T(256)}, u32[]{:S(2)}) %copy-start.4) | copy-done | bytes 1048
  4.1 31.1 %layer.1 = (bf16[128,256]{1,0:T(8,128)(2,1)S(1)}, f32[128,128]{1,0:T(8,128)S(1)}, f32[128,256]{1,0:T(8,128)S(1)}, f32[128,256]{1,0:T(8,128)S(1)}) custom-call(s32[256]{0:T(256)S(1)} %copy-done.4, s32[128,128,128]{2,1,0:T(8,128)} %counts.1, bf16[128,128]{1,0:T(8,128)(2,1)S(1)} %copy-done.3, s32[1,64]{1,0:T(1,128)S(1)} %bitcast.1, ...), custom_call_target="tpu_custom_call" | custom-call | tf_op jit(solution)/shard_map/layer/pallas_call | solution.py:305
  35.2 0.8 %finish.1 = (bf16[128,256]{1,0:T(8,128)(2,1)}, f32[128,128]{1,0:T(8,128)}, f32[128,256]{1,0:T(8,128)}, f32[128,256]{1,0:T(8,128)}) custom-call(bf16[128,256]{1,0:T(8,128)(2,1)S(1)} %get-tuple-element.8.refs_0_, f32[128,128]{1,0:T(8,128)S(1)} %get-tuple-element.9.refs_1_, f32[128,256]{1,0:T(8,128)S(1)} %get-tuple-element.10.refs_2_, ...), custom_call_target="tpu_custom_call" | custom-call | tf_op jit(solution)/shard_map/finish/pallas_call | solution.py:70
Async XLA Ops:
  0.6 2.7 %copy-start = (bf16[128,256]{1,0:T(8,128)(2,1)S(1)}, bf16[128,256]{1,0:T(8,128)(2,1)}, u32[]{:S(2)}) copy-start(bf16[128,256]{1,0:T(8,128)(2,1)} %cot.1) | copy-start | bytes 196612
  0.6 2.7 %copy-start.1 = (bf16[128,256]{1,0:T(8,128)(2,1)S(1)}, bf16[128,256]{1,0:T(8,128)(2,1)}, u32[]{:S(2)}) copy-start(bf16[128,256]{1,0:T(8,128)(2,1)} %ws.1) | copy-start | bytes 196612
  0.7 2.7 %copy-start.2 = (bf16[128,256]{1,0:T(8,128)(2,1)S(1)}, bf16[128,256]{1,0:T(8,128)(2,1)}, u32[]{:S(2)}) copy-start(bf16[128,256]{1,0:T(8,128)(2,1)} %wn.1) | copy-start | bytes 196612
  0.7 2.7 %copy-start.3 = (bf16[128,128]{1,0:T(8,128)(2,1)S(1)}, bf16[128,128]{1,0:T(8,128)(2,1)}, u32[]{:S(2)}) copy-start(bf16[128,128]{1,0:T(8,128)(2,1)} %feat.1) | copy-start | bytes 98308
  0.7 2.7 %copy-start.5 = (s32[64]{0:T(128)S(1)}, s32[64]{0:T(128)}, u32[]{:S(2)}) copy-start(s32[64]{0:T(128)} %param.12) | copy-start | bytes 772
  3.4 0.7 %copy-start.4 = (s32[256]{0:T(256)S(1)}, s32[256]{0:T(256)}, u32[]{:S(2)}) copy-start(s32[256]{0:T(256)} %slot_table.1.table) | copy-start | bytes 3076
